TPU v7x, 128 devices: a whole 4x4x4 slice. The times are simulated.
128 devices in a mesh: seq: 128 (over x, y, z, core).
Axes of the slice: x: 4, y: 4, z: 4, core: 2. Of those that a mesh axis runs over, the one named last changes fastest.
Arguments:
- inputs: bfloat16 [2, 32768, 1536], P(None, 'seq'), may hold values from -8 to 8
- ln_gain: float32 [1536], replicated, may hold values from 0.25 to 1.75
- w_in: bfloat16 [1536, 3072], replicated, may hold values from -0.15625 to 0.15625
- kernel: float32 [32, 1536], replicated, may hold values from -1 to 1
- bn_gain: float32 [1536], replicated, may hold values from 0.25 to 1.75
- bn_bias: float32 [1536], replicated, may hold values from -0.6 to 0.6
- w_out: bfloat16 [1536, 1536], replicated, may hold values from -0.15625 to 0.15625
- cotangent: bfloat16 [2, 32768, 1536], P(None, 'seq'), may hold values from -24 to 24
Outputs:
- outputs: bfloat16 [2, 32768, 1536], P(None, 'seq')
- d_inputs: bfloat16 [2, 32768, 1536], P(None, 'seq')
- d_w_out: float32 [1536, 1536], P('seq')
- d_kernel: float32 [32, 1536], replicated
- d_bn_gain: float32 [1536], replicated
- d_bn_bias: float32 [1536], replicated
All inputs are finite; a program needn't handle non-finite values.
Results may differ from a plain program's by a relative error of at most 0.0075.
Values may be sent and summed in bfloat16 or wider, within the bound.
A program may use at most 128 MiB of HBM per device.

v0:
```python
import jax
import jax.numpy as jnp
from jax import lax
from jax.sharding import PartitionSpec as P

D = 1536
K = 32
FRAMES_DEV = 256
UTT = 2
EPSILON = 1e-05


def with_halo(block, sides, width):
    for axis, dim in sides:
        count = lax.axis_size(axis)
        forward = [(i, i + 1) for i in range(count - 1)]
        backward = [(target, source) for source, target in forward]
        low = lax.ppermute(
            lax.slice_in_dim(block, block.shape[dim] - width, None, axis=dim), axis, forward
        )
        high = lax.ppermute(lax.slice_in_dim(block, 0, width, axis=dim), axis, backward)
        block = jnp.concatenate([low, block, high], axis=dim)
    return block


def on_device(inputs, ln_gain, w_in, kernel, bn_gain, bn_bias, w_out, cotangent):
    devices_seq = lax.axis_size("seq")
    frame_total = UTT * FRAMES_DEV * devices_seq
    rows_here = UTT * FRAMES_DEV
    x_float = inputs.astype(jnp.float32)
    ln_mean = jnp.mean(x_float, axis=-1, keepdims=True)
    centred = x_float - ln_mean
    ln_rstd = lax.rsqrt(jnp.mean(centred * centred, axis=-1, keepdims=True) + EPSILON)
    ln_hat = centred * ln_rstd
    normed = (ln_hat * ln_gain).astype(jnp.bfloat16).reshape(rows_here, D)
    proj = jnp.dot(normed, w_in, preferred_element_type=jnp.float32)
    value_half = proj[:, :D]
    gate_sig = jax.nn.sigmoid(proj[:, D:])
    gated = (value_half * gate_sig).astype(jnp.bfloat16).reshape(UTT, FRAMES_DEV, D)
    padded = with_halo(gated, (("seq", 1),), 16)
    conv_out = jnp.zeros((UTT, FRAMES_DEV, D), jnp.float32)
    for tap_index in range(K):
        conv_out = conv_out + kernel[tap_index] * padded[
            :, tap_index + 1 : tap_index + 1 + FRAMES_DEV
        ].astype(jnp.float32)
    bn_mean = lax.psum(jnp.sum(conv_out, axis=(0, 1)), "seq") / frame_total
    deviate = conv_out - bn_mean
    bn_var = lax.psum(jnp.sum(deviate * deviate, axis=(0, 1)), "seq") / frame_total
    bn_rstd = lax.rsqrt(bn_var + EPSILON)
    normed_bn = deviate * bn_rstd
    bn_out = normed_bn * bn_gain + bn_bias
    act_sig = jax.nn.sigmoid(bn_out)
    act = (bn_out * act_sig).astype(jnp.bfloat16).reshape(rows_here, D)
    branch = lax.dot_general(
        act, w_out, (((1,), (1,)), ((), ())), preferred_element_type=jnp.float32
    )
    outputs = (
        (x_float.reshape(rows_here, D) + branch).astype(jnp.bfloat16).reshape(UTT, FRAMES_DEV, D)
    )
    cot_rows = cotangent.reshape(rows_here, D)
    d_w_out = lax.psum_scatter(
        lax.dot_general(
            cot_rows, act, (((0,), (0,)), ((), ())), preferred_element_type=jnp.float32
        ),
        "seq",
        scatter_dimension=0,
        tiled=True,
    )
    d_act = jnp.dot(cot_rows, w_out, preferred_element_type=jnp.float32)
    d_bn = d_act.reshape(UTT, FRAMES_DEV, D) * (act_sig + bn_out * act_sig * (1.0 - act_sig))
    scaled_grad = d_bn * bn_gain
    local_bias = jnp.sum(d_bn, axis=(0, 1))
    local_gain = jnp.sum(d_bn * normed_bn, axis=(0, 1))
    d_bn_bias, d_bn_gain = lax.psum((local_bias, local_gain), "seq")
    mean_grad = bn_gain * d_bn_bias / frame_total
    mean_cross = bn_gain * d_bn_gain / frame_total
    d_conv = bn_rstd * (scaled_grad - mean_grad - normed_bn * mean_cross)
    kernel_rows = []
    for tap_index in range(K):
        window = padded[:, tap_index + 1 : tap_index + 1 + FRAMES_DEV].astype(jnp.float32)
        kernel_rows.append(jnp.sum(window * d_conv, axis=(0, 1)))
    d_kernel = lax.psum(jnp.stack(kernel_rows), "seq")
    grad_padded = with_halo(d_conv.astype(jnp.bfloat16), (("seq", 1),), 16).astype(d_conv.dtype)
    d_gated = jnp.zeros((UTT, FRAMES_DEV, D), jnp.float32)
    for tap_index in range(K):
        d_gated = (
            d_gated
            + kernel[tap_index] * grad_padded[:, 31 - tap_index : 31 - tap_index + FRAMES_DEV]
        )
    d_gated = d_gated.reshape(rows_here, D)
    d_value = d_gated * gate_sig
    d_gate = d_gated * value_half * gate_sig * (1.0 - gate_sig)
    d_proj = jnp.concatenate([d_value, d_gate], axis=-1).astype(jnp.bfloat16)
    d_normed = lax.dot_general(
        d_proj, w_in, (((1,), (1,)), ((), ())), preferred_element_type=jnp.float32
    )
    d_hat = d_normed.reshape(UTT, FRAMES_DEV, D) * ln_gain
    d_layer = ln_rstd * (
        d_hat
        - jnp.mean(d_hat, axis=-1, keepdims=True)
        - ln_hat * jnp.mean(d_hat * ln_hat, axis=-1, keepdims=True)
    )
    d_inputs = (cotangent.astype(jnp.float32) + d_layer).astype(jnp.bfloat16)
    return (outputs, d_inputs, d_w_out, d_kernel, d_bn_gain, d_bn_bias)


def solution(mesh):
    return jax.shard_map(
        on_device,
        mesh=mesh,
        in_specs=(P(None, "seq", None), P(), P(), P(), P(), P(), P(), P(None, "seq", None)),
        out_specs=(P(None, "seq", None), P(None, "seq", None), P("seq", None), P(), P(), P()),
        check_vma=False,
    )
```

profile of v0, /device:TPU:1, one launch (start us, length us, event | category | flops | bytes accessed | tf_op | source)
XLA Modules:
  0.0 475.8 jit_solution(6670448868981798242)
XLA Ops:
  9.1 2.0 multiply_reduce_fusion.4
  11.6 7.6 %fusion.148 = f32[512,3072]{1,0:T(8,128)S(1)} fusion(bf16[512,1536]{1,0:T(8,128)(2,1)S(1)} %bitcast.51, bf16[1536,3072]{1,0:T(8,128)(2,1)} %param.10), kind=kOutput, calls=%fused_computation.333 | convolution fusion | flops 4831838208 | bytes 17301504 | tf_op jit(solution)/shard_map/dot_general | solution.py:36
  22.5 3.3 collective-permute-start.1
  25.8 3.6 collective-permute-start
  31.3 17.2 %fusion.144 = (f32[1536]{0:T(1024)S(1)}, f32[2,256,1536]{2,1,0:T(8,128)}) fusion(bf16[2,16,1536]{2,1,0:T(8,128)(2,1)S(1)} %collective-permute-done.1, bf16[2,256,1536]{2,1,0:T(8,128)(2,1)S(1)} %bitcast.42, f32[1536]{0:T(1024)S(1)} %get-tuple-element.82, f32[1536]{0:T(1024)S(1)} %get-tuple-element.83, f32[1536]{0:T(1024)S(1)} %get-tuple-element.53, ...), kind=kLoop, calls=%fused_computation.330 | loop fusion | flops 148634112 | bytes 5117952 | tf_op jit(solution)/shard_map/reduce_sum | solution.py:46
  48.5 73.1 %psum.35 = f32[1536]{0:T(1024)S(1)} all-reduce(f32[1536]{0:T(1024)S(1)} %get-tuple-element.89), channel_id=1, replica_groups=mesh['seq'=128] {'seq'}, use_global_device_ids=true, to_apply=%region_3.0 | all-reduce | flops 1536 | bytes 12288 | tf_op jit(solution)/shard_map/psum | solution.py:46
  121.6 2.2 multiply_reduce_fusion.3
  123.8 64.1 %psum.36 = f32[1536]{0:T(1024)S(1)} all-reduce(f32[1536]{0:T(1024)S(1)} %multiply_reduce_fusion.3), channel_id=1, replica_groups=mesh['seq'=128] {'seq'}, use_global_device_ids=true, to_apply=%region_5.0 | all-reduce | flops 1536 | bytes 12288 | tf_op jit(solution)/shard_map/psum | solution.py:48
  188.0 9.6 %fusion.143 = (f32[1536]{0:T(1024)S(1)}, f32[1536]{0:T(1024)S(1)}, bf16[2,256,1536]{2,1,0:T(8,128)(2,1)}, f32[2,256,1536]{2,1,0:T(8,128)}) fusion(f32[1536]{0:T(1024)S(1)} %add_rsqrt_fusion, f32[2,256,1536]{2,1,0:T(8,128)} %get-tuple-element.90, f32[1536]{0:T(1024)S(1)} %broadcast_multiply_fusion, f32[1536]{0:T(1024)S(1)} %copy-done.60, ...), kind=kOutput, calls=%fused_computation.329 | convolution fusion | flops 2428498944 | bytes 14192640 | tf_op jit(solution)/shard_map/dot_general | solution.py:69
  197.6 63.0 %all-reduce.1 = (f32[1536]{0:T(1024)S(1)}, f32[1536]{0:T(1024)S(1)}) all-reduce(f32[1536]{0:T(1024)S(1)} %get-tuple-element.51, f32[1536]{0:T(1024)S(1)} %get-tuple-element.50), channel_id=1, replica_groups=mesh['seq'=128] {'seq'}, use_global_device_ids=true, to_apply=%region_9.0 | all-reduce | flops 3072 | bytes 24576 | tf_op jit(solution)/shard_map/psum | solution.py:74
  260.6 8.1 %fusion.67 = (f32[1536]{0:T(1024)S(1)}, f32[1536]{0:T(1024)S(1)}, f32[1536]{0:T(1024)S(1)}, f32[1536]{0:T(1024)S(1)}, f32[1536]{0:T(1024)S(1)}, /*index=5*/f32[1...) fusion(bf16[2,16,1536]{2,1,0:T(8,128)(2,1)S(1)} %collective-permute-done.1, ...), kind=kLoop, calls=%fused_computation.160 | loop fusion | flops 47958528 | bytes 11194368 | tf_op jit(solution)/shard_map/reduce_sum | solution.py:81
  268.8 7.1 %fusion.52 = (f32[1536]{0:T(1024)S(1)}, f32[1536]{0:T(1024)S(1)}, f32[1536]{0:T(1024)S(1)}, f32[1536]{0:T(1024)S(1)}, f32[1536]{0:T(1024)S(1)}, /*index=5*/f32[1...) fusion(f32[2,256,1536]{2,1,0:T(8,128)S(1)} %get-tuple-element.88, ...), kind=kLoop, calls=%fused_computation.145 | loop fusion | flops 40095744 | bytes 12730368 | tf_op jit(solution)/shard_map/reduce_sum | solution.py:81
  275.9 2.5 collective-permute-start.3
  278.4 3.1 collective-permute-start.2
  281.5 3.8 fusion.110
  285.3 2.8 fusion.35
  288.1 4.1 fusion.44
  292.2 5.1 %convolution_bitcast_fusion = f32[1536,1536]{0,1:T(8,128)} fusion(bf16[2,256,1536]{2,1,0:T(8,128)(2,1)S(1)} %copy-done.61, bf16[2,256,1536]{2,1,0:T(8,128)(2,1)S(1)} %copy-done.5), kind=kOutput, calls=%fused_computation.29 | convolution fusion | flops 2415919104 | bytes 12582912 | tf_op jit(solution)/shard_map/dot_general | solution.py:62
  297.7 2.8 stack.131
  303.7 12.4 %fusion.68 = f32[2,256,1536]{2,1,0:T(8,128)S(1)} fusion(f32[2,288,1536]{2,1,0:T(8,128)S(1)} %maximum_convert_fusion, f32[1536]{0:T(1024)S(1)} %copy-done.48, f32[1536]{0:T(1024)S(1)} %copy-done.50, f32[1536]{0:T(1024)S(1)} %get-tuple-element.53, f32[1536]{0:T(1024)S(1)} %copy-done.8, f32[1536]{0:T(1024)S(1)} %copy-done.9, f32[1536]{0:T(1024)S(1)} %copy-done.10, ...), kind=kLoop, calls=%fused_computation.162 | loop fusion | flops 49545216 | bytes 104005632 | tf_op jit(solution)/shard_map/add | solution.py:87
  317.8 9.2 %multiply_reduce_fusion.1 = (f32[512]{0:T(512)S(1)}, f32[512,1536]{1,0:T(8,128)}) fusion(f32[1536]{0:T(1024)S(1)} %copy-done.52, bf16[1536,3072]{1,0:T(8,128)(2,1)} %param.10, bf16[512,1536]{1,0:T(8,128)(2,1)S(1)} %get-tuple-element.92, bf16[512,1536]{1,0:T(8,128)(2,1)S(1)} %get-tuple-element.91), kind=kOutput, calls=%fused_computation.240 | convolution fusion | flops 4839702016 | bytes 15736832 | tf_op jit(solution)/shard_map/dot_general | solution.py:94
  327.1 2.9 multiply_reduce_fusion
  330.6 2.4 add_convert_fusion
  333.1 131.7 %all-reduce.5.cloned.1.call-done = (f32[1536,1536]{0,1:T(8,128)}, f32[32,1536]{1,0:T(8,128)}) async-done(((f32[1536,1536]{0,1:T(8,128)}, f32[32,1536]{1,0:T(8,128)}), (f32[1536,1536]{0,1:T(8,128)}, f32[32,1536]{1,0:T(8,128)})) %all-reduce.5.cloned.1.call-update) | async-done | bytes 9633808
  (192 shorter events, 17.0 us)
Async XLA Ops:
  7.2 457.6 %all-reduce.5.cloned.1.call-start = ((), (), s32[]{:S(2)}) async-start(), calls=%async_computation | async-start | bytes 19267584
  22.5 8.1 %collective-permute-start.1 = (bf16[2,16,1536]{2,1,0:T(8,128)(2,1)}, bf16[2,16,1536]{2,1,0:T(8,128)(2,1)S(1)}, u32[]{:S(2)}, u32[]{:S(2)}) collective-permute-start(bf16[2,16,1536]{2,1,0:T(8,128)(2,1)} %get-tuple-element.98), channel_id=1, source_target_pairs={{1,0},{2,1},{3,2},{4,3},{5,4},{6,5},{7,6},{8,7},{9,8},{10,9},{11,1... | collective-permute-start | bytes 294920 | tf_op jit(solution)/shard_map/ppermute | solution.py:21
  25.8 5.5 %collective-permute-start = (bf16[2,16,1536]{2,1,0:T(8,128)(2,1)}, bf16[2,16,1536]{2,1,0:T(8,128)(2,1)S(1)}, u32[]{:S(2)}, u32[]{:S(2)}) collective-permute-start(bf16[2,16,1536]{2,1,0:T(8,128)(2,1)} %get-tuple-element.97), channel_id=1, source_target_pairs={{0,1},{1,2},{2,3},{3,4},{4,5},{5,6},{6,7},{7,8},{8,9},{9,10},{10,1... | collective-permute-start | bytes 294920 | tf_op jit(solution)/shard_map/ppermute | solution.py:18
  30.5 17.9 %copy-start.27 = (f32[1536]{0:T(1024)}, f32[1536]{0:T(1024)S(1)}, u32[]{:S(2)}) copy-start(f32[1536]{0:T(1024)S(1)} %get-tuple-element.72) | copy-start | bytes 18436
  30.5 17.9 %copy-start.29 = (f32[1536]{0:T(1024)}, f32[1536]{0:T(1024)S(1)}, u32[]{:S(2)}) copy-start(f32[1536]{0:T(1024)S(1)} %get-tuple-element.73) | copy-start | bytes 18436
  30.5 17.9 %copy-start.31 = (f32[1536]{0:T(1024)}, f32[1536]{0:T(1024)S(1)}, u32[]{:S(2)}) copy-start(f32[1536]{0:T(1024)S(1)} %get-tuple-element.74) | copy-start | bytes 18436
  30.5 17.9 %copy-start.33 = (f32[1536]{0:T(1024)}, f32[1536]{0:T(1024)S(1)}, u32[]{:S(2)}) copy-start(f32[1536]{0:T(1024)S(1)} %get-tuple-element.75) | copy-start | bytes 18436
  30.5 17.9 %copy-start.35 = (f32[1536]{0:T(1024)}, f32[1536]{0:T(1024)S(1)}, u32[]{:S(2)}) copy-start(f32[1536]{0:T(1024)S(1)} %get-tuple-element.76) | copy-start | bytes 18436
  30.5 17.9 %copy-start.37 = (f32[1536]{0:T(1024)}, f32[1536]{0:T(1024)S(1)}, u32[]{:S(2)}) copy-start(f32[1536]{0:T(1024)S(1)} %get-tuple-element.77) | copy-start | bytes 18436
  30.5 17.9 %copy-start.39 = (f32[1536]{0:T(1024)}, f32[1536]{0:T(1024)S(1)}, u32[]{:S(2)}) copy-start(f32[1536]{0:T(1024)S(1)} %get-tuple-element.78) | copy-start | bytes 18436
  30.6 17.9 %copy-start.41 = (f32[1536]{0:T(1024)}, f32[1536]{0:T(1024)S(1)}, u32[]{:S(2)}) copy-start(f32[1536]{0:T(1024)S(1)} %get-tuple-element.79) | copy-start | bytes 18436
  30.6 17.9 %copy-start.43 = (f32[1536]{0:T(1024)}, f32[1536]{0:T(1024)S(1)}, u32[]{:S(2)}) copy-start(f32[1536]{0:T(1024)S(1)} %get-tuple-element.80) | copy-start | bytes 18436
  30.6 17.9 %copy-start.45 = (f32[1536]{0:T(1024)}, f32[1536]{0:T(1024)S(1)}, u32[]{:S(2)}) copy-start(f32[1536]{0:T(1024)S(1)} %get-tuple-element.81) | copy-start | bytes 18436
  30.6 17.9 %copy-start.47 = (f32[1536]{0:T(1024)}, f32[1536]{0:T(1024)S(1)}, u32[]{:S(2)}) copy-start(f32[1536]{0:T(1024)S(1)} %get-tuple-element.82) | copy-start | bytes 18436
  30.6 17.9 %copy-start.49 = (f32[1536]{0:T(1024)}, f32[1536]{0:T(1024)S(1)}, u32[]{:S(2)}) copy-start(f32[1536]{0:T(1024)S(1)} %get-tuple-element.83) | copy-start | bytes 18436
  31.3 156.7 %copy-start.57 = (f32[1536]{0:T(1024)S(1)}, f32[1536]{0:T(1024)}, u32[]{:S(2)}) copy-start(f32[1536]{0:T(1024)} %param.12) | copy-start | bytes 18436
  31.3 156.7 %copy-start.60 = (f32[1536]{0:T(1024)S(1)}, f32[1536]{0:T(1024)}, u32[]{:S(2)}) copy-start(f32[1536]{0:T(1024)} %param.13) | copy-start | bytes 18436
  260.6 20.9 %slice-start.2 = ((s8[4718592]{0:T(1024)(128)(4,1)}), s8[4194304]{0:T(1024)(128)(4,1)S(1)}, s32[]{:S(2)}) async-start(s8[4718592]{0:T(1024)(128)(4,1)} %bitcast.52), calls=%async_computation.3 | async-start | bytes 8388608
  268.8 12.7 %slice-start.3 = ((s8[4718592]{0:T(1024)(128)(4,1)}), s8[524288]{0:T(1024)(128)(4,1)S(1)}, s32[]{:S(2)}) async-start(s8[4718592]{0:T(1024)(128)(4,1)} %bitcast.52), calls=%async_computation.4 | async-start | bytes 1048576
  268.8 12.7 %copy-start.61 = (bf16[2,256,1536]{2,1,0:T(8,128)(2,1)S(1)}, bf16[2,256,1536]{2,1,0:T(8,128)(2,1)}, u32[]{:S(2)}) copy-start(bf16[2,256,1536]{2,1,0:T(8,128)(2,1)} %get-tuple-element.93) | copy-start | bytes 4718596
  275.9 24.9 %collective-permute-start.3 = (bf16[2,16,1536]{2,1,0:T(8,128)(2,1)S(1)}, bf16[2,16,1536]{2,1,0:T(8,128)(2,1)S(1)}, u32[]{:S(2)}, u32[]{:S(2)}) collective-permute-start(bf16[2,16,1536]{2,1,0:T(8,128)(2,1)S(1)} %get-tuple-element.96), channel_id=1, source_target_pairs={{1,0},{2,1},{3,2},{4,3},{5,4},{6,5},{7,6},{8,7},{9,8},{10,9},{11,1... | collective-permute-start | bytes 294920 | tf_op jit(solution)/shard_map/ppermute | solution.py:21
  278.4 22.4 %collective-permute-start.2 = (bf16[2,16,1536]{2,1,0:T(8,128)(2,1)S(1)}, bf16[2,16,1536]{2,1,0:T(8,128)(2,1)}, u32[]{:S(2)}, u32[]{:S(2)}) collective-permute-start(bf16[2,16,1536]{2,1,0:T(8,128)(2,1)S(1)} %get-tuple-element.95), channel_id=1, source_target_pairs={{0,1},{1,2},{2,3},{3,4},{4,5},{5,6},{6,7},{7,8},{8,9},{9,10},{10,1... | collective-permute-start | bytes 294920 | tf_op jit(solution)/shard_map/ppermute | solution.py:18
  301.9 14.2 %slice-start = ((s8[6291456]{0:T(1024)(128)(4,1)}), s8[4194304]{0:T(1024)(128)(4,1)S(1)}, s32[]{:S(2)}) async-start(s8[6291456]{0:T(1024)(128)(4,1)} %bitcast.47), calls=%async_computation.1 | async-start | bytes 8388608
  303.7 12.4 %slice-start.1 = ((s8[6291456]{0:T(1024)(128)(4,1)}), s8[2097152]{0:T(1024)(128)(4,1)S(1)}, s32[]{:S(2)}) async-start(s8[6291456]{0:T(1024)(128)(4,1)} %bitcast.47), calls=%async_computation.2 | async-start | bytes 4194304
  (47 other events, 169.3 us)
Sparse Core Ops, SparseCore 0:
  300.6 164.0 all-reduce.4
where the time goes:
time: 477 us; the launch traced here: 476 us
  blocking collectives  200 us (42%)
  waiting for transfers between devices  132 us (28%)
  other arithmetic  67.4 us (14%)
  matrix products  35.3 us (7%)
  between operations  15.4 us (3%)
  local copies, waits for them, and re-layouts  12.7 us (3%)
  starting transfers between devices  12.4 us (3%)
    unnamed x2, waiting for transfers between devices  132 us
    psum x1, blocking collectives, on_device(): bn_mean = lax.psum(jnp.sum(conv_out, axis=(0, 1)), 'seq') / frame_total  73.1 us
    psum x1, blocking collectives, on_device(): lax.psum(jnp.sum(deviate * deviate, axis=(0, 1)), 'seq') / frame_total  64.1 us
    psum x1, blocking collectives, on_device(): d_bn_bias, d_bn_gain = lax.psum((local_bias, local_gain), 'seq')  63 us
    reduce_sum x4, other arithmetic, on_device(): kernel_rows.append(jnp.sum(window * d_conv, axis=(0, 1)))  22 us
    reduce_sum x1, other arithmetic, on_device(): bn_mean = lax.psum(jnp.sum(conv_out, axis=(0, 1)), 'seq') / frame_total  17.2 us
    add x1, other arithmetic, on_device(): d_gated + kernel[tap_index] * grad_padded[:, 31 - tap_index:31 - tap_inde...  12.4 us
    dot_general x1, matrix products, on_device(): d_act = jnp.dot(cot_rows, w_out, preferred_element_type=jnp.float32)  9.63 us
  transfers between devices with their start and end apart: 5, of which 2 were waited for; matrix products, arithmetic and copies ran while one was open for 10% of the time, Pallas kernels for 0%

commit v1 on v0

--- a/solution.py
+++ b/solution.py
@@ -43,7 +43,7 @@
         conv_out = conv_out + kernel[tap_index] * padded[
             :, tap_index + 1 : tap_index + 1 + FRAMES_DEV
         ].astype(jnp.float32)
-    bn_mean = lax.psum(jnp.sum(conv_out, axis=(0, 1)), "seq") / frame_total
+    bn_mean = jnp.sum(lax.all_gather(jnp.sum(conv_out, axis=(0, 1)), "seq"), axis=0) / frame_total
     deviate = conv_out - bn_mean
     bn_var = lax.psum(jnp.sum(deviate * deviate, axis=(0, 1)), "seq") / frame_total
     bn_rstd = lax.rsqrt(bn_var + EPSILON)

time: 477 us -> 454 us (0.952)
  blocking collectives: 200 us -> 175 us
    psum x1 -> x0, blocking collectives: 73.1 us -> none  [on_device(): bn_mean = lax.psum(jnp.sum(conv_out, axis=(0, 1)), 'seq') / frame_total]
    all_gather x0 -> x1, blocking collectives: none -> 48.3 us  [on_device(): lax.all_gather(jnp.sum(conv_out, axis=(0, 1)), 'seq')]
    reduce_sum x1 -> x2, other arithmetic: 17.2 us -> 18.8 us  [the longest x1 17.2 us: on_device(): jnp.sum(conv_out, axis=(0, 1))]
  transfers between devices with their start and end apart: 5 -> 5, of which waited for: 2 -> 2; matrix products, arithmetic and copies ran while one was open for 10% -> 11% of each run, Pallas kernels for 0% -> 0%
where the time goes in v1:
time: 454 us; the launch traced here: 453 us
  blocking collectives  175 us (39%)
  waiting for transfers between devices  132 us (29%)
  other arithmetic  69.1 us (15%)
  matrix products  35.3 us (8%)
  between operations  15.4 us (3%)
  local copies, waits for them, and re-layouts  12.8 us (3%)
  starting transfers between devices  12.7 us (3%)
    unnamed x2, waiting for transfers between devices  132 us
    psum x1, blocking collectives, on_device(): lax.psum(jnp.sum(deviate * deviate, axis=(0, 1)), 'seq') / frame_total  64.3 us
    psum x1, blocking collectives, on_device(): d_bn_bias, d_bn_gain = lax.psum((local_bias, local_gain), 'seq')  62.8 us
    all_gather x1, blocking collectives, on_device(): lax.all_gather(jnp.sum(conv_out, axis=(0, 1)), 'seq')  48.3 us
    reduce_sum x4, other arithmetic, on_device(): kernel_rows.append(jnp.sum(window * d_conv, axis=(0, 1)))  22 us
    reduce_sum x1, other arithmetic, on_device(): jnp.sum(conv_out, axis=(0, 1))  17.2 us
    add x1, other arithmetic, on_device(): d_gated + kernel[tap_index] * grad_padded[:, 31 - tap_index:31 - tap_inde...  12.4 us
    dot_general x1, matrix products, on_device(): d_act = jnp.dot(cot_rows, w_out, preferred_element_type=jnp.float32)  9.63 us
  transfers between devices with their start and end apart: 5, of which 2 were waited for; matrix products, arithmetic and copies ran while one was open for 11% of the time, Pallas kernels for 0%

profile of v1, /device:TPU:1, one launch (start us, length us, event | category | flops | bytes accessed | tf_op | source)
XLA Modules:
  0.0 452.8 jit_solution(14320021581299311621)
XLA Ops:
  9.1 2.0 multiply_reduce_fusion.4
  11.6 7.6 %fusion.148 = f32[512,3072]{1,0:T(8,128)S(1)} fusion(bf16[512,1536]{1,0:T(8,128)(2,1)S(1)} %bitcast.51, bf16[1536,3072]{1,0:T(8,128)(2,1)} %param.10), kind=kOutput, calls=%fused_computation.333 | convolution fusion | flops 4831838208 | bytes 17301504 | tf_op jit(solution)/shard_map/dot_general | solution.py:36
  22.5 3.3 collective-permute-start.1
  25.8 3.6 collective-permute-start
  31.3 17.2 %fusion.144 = (f32[1536]{0:T(1024)S(1)}, f32[2,256,1536]{2,1,0:T(8,128)}) fusion(bf16[2,16,1536]{2,1,0:T(8,128)(2,1)S(1)} %collective-permute-done.1, bf16[2,256,1536]{2,1,0:T(8,128)(2,1)S(1)} %bitcast.42, f32[1536]{0:T(1024)S(1)} %get-tuple-element.82, f32[1536]{0:T(1024)S(1)} %get-tuple-element.83, f32[1536]{0:T(1024)S(1)} %get-tuple-element.53, ...), kind=kLoop, calls=%fused_computation.330 | loop fusion | flops 148634112 | bytes 5117952 | tf_op jit(solution)/shard_map/reduce_sum | solution.py:46
  48.6 48.3 %all-gather.1 = f32[128,1,1536]{2,1,0:T(1,128)} all-gather(f32[1,1,1536]{2,1,0:T(1,128)S(1)} %reshape.112), channel_id=2, replica_groups=mesh['seq'=128] {'seq'}, dimensions={0}, use_global_device_ids=true | all-gather | bytes 792576 | tf_op jit(solution)/shard_map/all_gather | solution.py:46
  98.5 2.2 multiply_reduce_fusion.3
  100.7 64.3 %psum.28 = f32[1536]{0:T(1024)S(1)} all-reduce(f32[1536]{0:T(1024)S(1)} %multiply_reduce_fusion.3), channel_id=1, replica_groups=mesh['seq'=128] {'seq'}, use_global_device_ids=true, to_apply=%region_5.0 | all-reduce | flops 1536 | bytes 12288 | tf_op jit(solution)/shard_map/psum | solution.py:48
  165.0 9.6 %fusion.143 = (f32[1536]{0:T(1024)S(1)}, f32[1536]{0:T(1024)S(1)}, bf16[2,256,1536]{2,1,0:T(8,128)(2,1)}, f32[2,256,1536]{2,1,0:T(8,128)}) fusion(f32[1536]{0:T(1024)S(1)} %add_rsqrt_fusion, f32[2,256,1536]{2,1,0:T(8,128)} %get-tuple-element.90, f32[1536]{0:T(1024)S(1)} %broadcast_multiply_fusion, f32[1536]{0:T(1024)S(1)} %copy-done.60, ...), kind=kOutput, calls=%fused_computation.329 | convolution fusion | flops 2428498944 | bytes 14192640 | tf_op jit(solution)/shard_map/dot_general | solution.py:69
  174.7 62.8 %all-reduce.1 = (f32[1536]{0:T(1024)S(1)}, f32[1536]{0:T(1024)S(1)}) all-reduce(f32[1536]{0:T(1024)S(1)} %get-tuple-element.51, f32[1536]{0:T(1024)S(1)} %get-tuple-element.50), channel_id=1, replica_groups=mesh['seq'=128] {'seq'}, use_global_device_ids=true, to_apply=%region_9.0 | all-reduce | flops 3072 | bytes 24576 | tf_op jit(solution)/shard_map/psum | solution.py:74
  237.5 8.1 %fusion.67 = (f32[1536]{0:T(1024)S(1)}, f32[1536]{0:T(1024)S(1)}, f32[1536]{0:T(1024)S(1)}, f32[1536]{0:T(1024)S(1)}, f32[1536]{0:T(1024)S(1)}, /*index=5*/f32[1...) fusion(bf16[2,16,1536]{2,1,0:T(8,128)(2,1)S(1)} %collective-permute-done.1, ...), kind=kLoop, calls=%fused_computation.160 | loop fusion | flops 47958528 | bytes 11194368 | tf_op jit(solution)/shard_map/reduce_sum | solution.py:81
  245.7 7.1 %fusion.52 = (f32[1536]{0:T(1024)S(1)}, f32[1536]{0:T(1024)S(1)}, f32[1536]{0:T(1024)S(1)}, f32[1536]{0:T(1024)S(1)}, f32[1536]{0:T(1024)S(1)}, /*index=5*/f32[1...) fusion(f32[2,256,1536]{2,1,0:T(8,128)S(1)} %get-tuple-element.88, ...), kind=kLoop, calls=%fused_computation.145 | loop fusion | flops 40095744 | bytes 12730368 | tf_op jit(solution)/shard_map/reduce_sum | solution.py:81
  252.8 2.5 collective-permute-start.3
  255.2 3.3 collective-permute-start.2
  258.6 3.8 fusion.110
  262.4 2.8 fusion.35
  265.2 4.1 fusion.44
  269.3 5.1 %convolution_bitcast_fusion = f32[1536,1536]{0,1:T(8,128)} fusion(bf16[2,256,1536]{2,1,0:T(8,128)(2,1)S(1)} %copy-done.61, bf16[2,256,1536]{2,1,0:T(8,128)(2,1)S(1)} %copy-done.5), kind=kOutput, calls=%fused_computation.29 | convolution fusion | flops 2415919104 | bytes 12582912 | tf_op jit(solution)/shard_map/dot_general | solution.py:62
  274.8 2.8 stack.131
  280.8 12.4 %fusion.68 = f32[2,256,1536]{2,1,0:T(8,128)S(1)} fusion(f32[2,288,1536]{2,1,0:T(8,128)S(1)} %maximum_convert_fusion, f32[1536]{0:T(1024)S(1)} %copy-done.48, f32[1536]{0:T(1024)S(1)} %copy-done.50, f32[1536]{0:T(1024)S(1)} %get-tuple-element.53, f32[1536]{0:T(1024)S(1)} %copy-done.8, f32[1536]{0:T(1024)S(1)} %copy-done.9, f32[1536]{0:T(1024)S(1)} %copy-done.10, ...), kind=kLoop, calls=%fused_computation.162 | loop fusion | flops 49545216 | bytes 104005632 | tf_op jit(solution)/shard_map/add | solution.py:87
  294.9 9.2 %multiply_reduce_fusion.1 = (f32[512]{0:T(512)S(1)}, f32[512,1536]{1,0:T(8,128)}) fusion(f32[1536]{0:T(1024)S(1)} %copy-done.52, bf16[1536,3072]{1,0:T(8,128)(2,1)} %param.10, bf16[512,1536]{1,0:T(8,128)(2,1)S(1)} %get-tuple-element.92, bf16[512,1536]{1,0:T(8,128)(2,1)S(1)} %get-tuple-element.91), kind=kOutput, calls=%fused_computation.240 | convolution fusion | flops 4839702016 | bytes 15736832 | tf_op jit(solution)/shard_map/dot_general | solution.py:94
  304.1 3.0 multiply_reduce_fusion
  307.8 2.4 add_convert_fusion
  310.2 131.6 %all-reduce.5.cloned.1.call-done = (f32[1536,1536]{0,1:T(8,128)}, f32[32,1536]{1,0:T(8,128)}) async-done(((f32[1536,1536]{0,1:T(8,128)}, f32[32,1536]{1,0:T(8,128)}), (f32[1536,1536]{0,1:T(8,128)}, f32[32,1536]{1,0:T(8,128)})) %all-reduce.5.cloned.1.call-update) | async-done | bytes 9633808
  (194 shorter events, 18.6 us)
Async XLA Ops:
  7.2 434.6 %all-reduce.5.cloned.1.call-start = ((), (), s32[]{:S(2)}) async-start(), calls=%async_computation | async-start | bytes 19267584
  22.5 8.1 %collective-permute-start.1 = (bf16[2,16,1536]{2,1,0:T(8,128)(2,1)}, bf16[2,16,1536]{2,1,0:T(8,128)(2,1)S(1)}, u32[]{:S(2)}, u32[]{:S(2)}) collective-permute-start(bf16[2,16,1536]{2,1,0:T(8,128)(2,1)} %get-tuple-element.98), channel_id=1, source_target_pairs={{1,0},{2,1},{3,2},{4,3},{5,4},{6,5},{7,6},{8,7},{9,8},{10,9},{11,1... | collective-permute-start | bytes 294920 | tf_op jit(solution)/shard_map/ppermute | solution.py:21
  25.8 5.5 %collective-permute-start = (bf16[2,16,1536]{2,1,0:T(8,128)(2,1)}, bf16[2,16,1536]{2,1,0:T(8,128)(2,1)S(1)}, u32[]{:S(2)}, u32[]{:S(2)}) collective-permute-start(bf16[2,16,1536]{2,1,0:T(8,128)(2,1)} %get-tuple-element.97), channel_id=1, source_target_pairs={{0,1},{1,2},{2,3},{3,4},{4,5},{5,6},{6,7},{7,8},{8,9},{9,10},{10,1... | collective-permute-start | bytes 294920 | tf_op jit(solution)/shard_map/ppermute | solution.py:18
  30.5 17.9 %copy-start.27 = (f32[1536]{0:T(1024)}, f32[1536]{0:T(1024)S(1)}, u32[]{:S(2)}) copy-start(f32[1536]{0:T(1024)S(1)} %get-tuple-element.72) | copy-start | bytes 18436
  30.5 18.0 %copy-start.29 = (f32[1536]{0:T(1024)}, f32[1536]{0:T(1024)S(1)}, u32[]{:S(2)}) copy-start(f32[1536]{0:T(1024)S(1)} %get-tuple-element.73) | copy-start | bytes 18436
  30.5 18.0 %copy-start.31 = (f32[1536]{0:T(1024)}, f32[1536]{0:T(1024)S(1)}, u32[]{:S(2)}) copy-start(f32[1536]{0:T(1024)S(1)} %get-tuple-element.74) | copy-start | bytes 18436
  30.5 18.0 %copy-start.33 = (f32[1536]{0:T(1024)}, f32[1536]{0:T(1024)S(1)}, u32[]{:S(2)}) copy-start(f32[1536]{0:T(1024)S(1)} %get-tuple-element.75) | copy-start | bytes 18436
  30.5 18.0 %copy-start.35 = (f32[1536]{0:T(1024)}, f32[1536]{0:T(1024)S(1)}, u32[]{:S(2)}) copy-start(f32[1536]{0:T(1024)S(1)} %get-tuple-element.76) | copy-start | bytes 18436
  30.5 18.0 %copy-start.37 = (f32[1536]{0:T(1024)}, f32[1536]{0:T(1024)S(1)}, u32[]{:S(2)}) copy-start(f32[1536]{0:T(1024)S(1)} %get-tuple-element.77) | copy-start | bytes 18436
  30.5 18.0 %copy-start.39 = (f32[1536]{0:T(1024)}, f32[1536]{0:T(1024)S(1)}, u32[]{:S(2)}) copy-start(f32[1536]{0:T(1024)S(1)} %get-tuple-element.78) | copy-start | bytes 18436
  30.6 18.0 %copy-start.41 = (f32[1536]{0:T(1024)}, f32[1536]{0:T(1024)S(1)}, u32[]{:S(2)}) copy-start(f32[1536]{0:T(1024)S(1)} %get-tuple-element.79) | copy-start | bytes 18436
  30.6 18.0 %copy-start.43 = (f32[1536]{0:T(1024)}, f32[1536]{0:T(1024)S(1)}, u32[]{:S(2)}) copy-start(f32[1536]{0:T(1024)S(1)} %get-tuple-element.80) | copy-start | bytes 18436
  30.6 18.0 %copy-start.45 = (f32[1536]{0:T(1024)}, f32[1536]{0:T(1024)S(1)}, u32[]{:S(2)}) copy-start(f32[1536]{0:T(1024)S(1)} %get-tuple-element.81) | copy-start | bytes 18436
  30.6 18.0 %copy-start.47 = (f32[1536]{0:T(1024)}, f32[1536]{0:T(1024)S(1)}, u32[]{:S(2)}) copy-start(f32[1536]{0:T(1024)S(1)} %get-tuple-element.82) | copy-start | bytes 18436
  30.6 18.0 %copy-start.49 = (f32[1536]{0:T(1024)}, f32[1536]{0:T(1024)S(1)}, u32[]{:S(2)}) copy-start(f32[1536]{0:T(1024)S(1)} %get-tuple-element.83) | copy-start | bytes 18436
  48.4 116.6 %copy-start.57 = (f32[1536]{0:T(1024)S(1)}, f32[1536]{0:T(1024)}, u32[]{:S(2)}) copy-start(f32[1536]{0:T(1024)} %param.12) | copy-start | bytes 18436
  48.4 116.6 %copy-start.60 = (f32[1536]{0:T(1024)S(1)}, f32[1536]{0:T(1024)}, u32[]{:S(2)}) copy-start(f32[1536]{0:T(1024)} %param.13) | copy-start | bytes 18436
  237.5 21.1 %slice-start.2 = ((s8[4718592]{0:T(1024)(128)(4,1)}), s8[4194304]{0:T(1024)(128)(4,1)S(1)}, s32[]{:S(2)}) async-start(s8[4718592]{0:T(1024)(128)(4,1)} %bitcast.52), calls=%async_computation.3 | async-start | bytes 8388608
  245.6 12.9 %slice-start.3 = ((s8[4718592]{0:T(1024)(128)(4,1)}), s8[524288]{0:T(1024)(128)(4,1)S(1)}, s32[]{:S(2)}) async-start(s8[4718592]{0:T(1024)(128)(4,1)} %bitcast.52), calls=%async_computation.4 | async-start | bytes 1048576
  245.6 12.9 %copy-start.61 = (bf16[2,256,1536]{2,1,0:T(8,128)(2,1)S(1)}, bf16[2,256,1536]{2,1,0:T(8,128)(2,1)}, u32[]{:S(2)}) copy-start(bf16[2,256,1536]{2,1,0:T(8,128)(2,1)} %get-tuple-element.93) | copy-start | bytes 4718596
  252.8 25.2 %collective-permute-start.3 = (bf16[2,16,1536]{2,1,0:T(8,128)(2,1)S(1)}, bf16[2,16,1536]{2,1,0:T(8,128)(2,1)S(1)}, u32[]{:S(2)}, u32[]{:S(2)}) collective-permute-start(bf16[2,16,1536]{2,1,0:T(8,128)(2,1)S(1)} %get-tuple-element.96), channel_id=1, source_target_pairs={{1,0},{2,1},{3,2},{4,3},{5,4},{6,5},{7,6},{8,7},{9,8},{10,9},{11,1... | collective-permute-start | bytes 294920 | tf_op jit(solution)/shard_map/ppermute | solution.py:21
  255.2 22.7 %collective-permute-start.2 = (bf16[2,16,1536]{2,1,0:T(8,128)(2,1)S(1)}, bf16[2,16,1536]{2,1,0:T(8,128)(2,1)}, u32[]{:S(2)}, u32[]{:S(2)}) collective-permute-start(bf16[2,16,1536]{2,1,0:T(8,128)(2,1)S(1)} %get-tuple-element.95), channel_id=1, source_target_pairs={{0,1},{1,2},{2,3},{3,4},{4,5},{5,6},{6,7},{7,8},{8,9},{9,10},{10,1... | collective-permute-start | bytes 294920 | tf_op jit(solution)/shard_map/ppermute | solution.py:18
  279.0 14.2 %slice-start = ((s8[6291456]{0:T(1024)(128)(4,1)}), s8[4194304]{0:T(1024)(128)(4,1)S(1)}, s32[]{:S(2)}) async-start(s8[6291456]{0:T(1024)(128)(4,1)} %bitcast.47), calls=%async_computation.1 | async-start | bytes 8388608
  280.8 12.4 %slice-start.1 = ((s8[6291456]{0:T(1024)(128)(4,1)}), s8[2097152]{0:T(1024)(128)(4,1)S(1)}, s32[]{:S(2)}) async-start(s8[6291456]{0:T(1024)(128)(4,1)} %bitcast.47), calls=%async_computation.2 | async-start | bytes 4194304
  (47 other events, 169.6 us)
Sparse Core Ops, SparseCore 0:
  277.7 164.0 all-reduce.4
